TPU v7x, 32 devices: a whole 2x2x4 slice. The times are simulated.
32 devices in a mesh: grp: 2 (over y), pulse: 16 (over z, x, core), rng: 1.
Axes of the slice: x: 2, y: 2, z: 4, core: 2. Of those that a mesh axis runs over, the one named last changes fastest.
Arguments:
- raw_echoes: bfloat16 [256, 64, 2, 128], P(('grp', 'pulse'), 'rng'), parts along dimension 0, may hold values from -6 to 6
- matched: float32 [2, 128], replicated, may hold values from -0.375 to 0.375
- delays: int32 [256, 16], P(('grp', 'pulse')), parts along dimension 0, may hold values from -24 to 24
- pulse_phase: float32 [256, 16], P(('grp', 'pulse')), parts along dimension 0, may hold values from -3.140625 to 3.140625
- beam_map: int32 [4, 2, 2, 16], replicated, may hold values from 0 to 15, as said below
- range_shift: int32 [4, 2, 2, 16], replicated, may hold values from -24 to 24
- phase_base: float32 [4, 2, 2, 16], replicated, may hold values from -3.140625 to 3.140625
- phase_rate: float32 [4, 2, 2, 16], replicated, may hold values from -4 to 4
- tap_offsets: int32 [4, 4], replicated, may hold values from -4 to 4, as said below
Outputs:
- final_image: float32 [2, 512, 8192], P(None, ('grp', 'pulse'), 'rng'), parts along dimension 1
There are 2 independent parts, one for each index of `grp`. A program takes and returns all parts, laid end to end along the dimension named above; an argument that names none is the same for every part. Nothing has to cross between parts.
Inputs may be any that keep to these rules, and one draw needn't show every extreme that they name: `beam_map`: entry [l, h, s, k] is h * 8 + k // 2 plus -1, 0 or 1, clamped to the range. `tap_offsets`: the 4 entries of one level are distinct.
All inputs are finite; a program needn't handle non-finite values.
Results may differ from a plain program's by a relative error of at most 0.0055.
Values may be sent and summed in bfloat16 or wider, within the bound.
A program may use at most 64 MiB of HBM per device.

v0:
```python
import math

import jax
import jax.numpy as jnp
from jax import lax
from jax.sharding import PartitionSpec as P

R = 8192
BLOCK = 256
LEVELS = 4
SHIFT = 24
SPREAD = 4


SQRT_HALF = 0.7071067811865476


def shifted(array, axis, by):
    count = lax.axis_size(axis)
    pairs = [(i, i + by) for i in range(count) if 0 <= i + by < count]
    return lax.ppermute(array, axis, pairs)


def padded_2(block, sides, width):
    for axis, dim in sides:
        count = lax.axis_size(axis)
        forward = [(i, i + 1) for i in range(count - 1)]
        backward = [(target, source) for source, target in forward]
        low = lax.ppermute(
            lax.slice_in_dim(block, block.shape[dim] - width, None, axis=dim), axis, forward
        )
        high = lax.ppermute(lax.slice_in_dim(block, 0, width, axis=dim), axis, backward)
        block = jnp.concatenate([low, block, high], axis=dim)
    return block


def from_partner(block, axis, bit):
    count = lax.axis_size(axis)
    route = []
    for low in range(count):
        high = low | 1 << bit
        if high != low and high < count:
            route += [(low, high), (high, low)]
    return lax.ppermute(block, axis, route)


def tables(length):
    counter = jnp.arange(length, dtype=jnp.int32)
    product = counter[:, None] * counter[None, :] % length
    angles = product.astype(jnp.float32) * (2.0 * math.pi / length)
    cosine = jnp.cos(angles)
    sine_part = jnp.sin(angles)
    forward = jnp.concatenate(
        [
            jnp.concatenate([cosine, -sine_part], axis=1),
            jnp.concatenate([sine_part, cosine], axis=1),
        ],
        axis=0,
    )
    inverse = jnp.concatenate(
        [
            jnp.concatenate([cosine, sine_part], axis=1),
            jnp.concatenate([-sine_part, cosine], axis=1),
        ],
        axis=0,
    )
    return (forward, inverse)


def compress(echoes, tail, matched, forward_exact, forward, inverse_kept):
    pulses, blocks, parts, hop_bins = echoes.shape
    length = 2 * hop_bins
    previous = jnp.concatenate([tail[:, None], echoes[:, :-1]], axis=1)
    windows = jnp.concatenate([previous, echoes], axis=3).reshape(pulses * blocks, parts * length)
    taps_padded = jnp.concatenate(
        [matched, jnp.zeros((2, length - hop_bins), jnp.float32)], axis=1
    ).reshape(1, 2 * length)
    response = jnp.dot(taps_padded, forward_exact, precision=lax.Precision.HIGHEST)[0]
    resp_real = response[:length]
    resp_imag = response[length:]
    spectrum = jnp.dot(windows, forward, preferred_element_type=jnp.float32)
    spec_real = spectrum[:, :length]
    spec_imag = spectrum[:, length:]
    filt_real = spec_real * resp_real - spec_imag * resp_imag
    filt_imag = spec_real * resp_imag + spec_imag * resp_real
    shaped = jnp.concatenate([filt_real, filt_imag], axis=1).astype(jnp.bfloat16)
    restored = jnp.dot(shaped, inverse_kept, preferred_element_type=jnp.float32) * (1.0 / length)
    return restored.astype(jnp.bfloat16).reshape(pulses, blocks, parts, hop_bins)


def kept_columns(inverse, length):
    half = length // 2
    return jnp.concatenate([inverse[:, half:length], inverse[:, length + half :]], axis=1)


def inside_mask(first_cell, out_cells):
    global_cells = first_cell + jnp.arange(out_cells, dtype=jnp.int32)
    return ((global_cells >= 0) & (global_cells < R)).astype(jnp.float32)


def row_slices(rows, starts, width):

    def per_pulse(row, start_row):
        return jax.vmap(lambda start: lax.dynamic_slice_in_dim(row, start, width, 1))(start_row)

    return jax.vmap(per_pulse)(rows, starts)


def project(padded, delay_rows, phase_rows, offset_base, out_cells, first_cell):
    pulses = padded.shape[0]
    beam_count = delay_rows.shape[1]
    group_size = math.gcd(pulses, 4)
    block_count = pulses // group_size

    def accumulate(summed, block_index):
        first_row = block_index * group_size
        pulses_block = lax.dynamic_slice_in_dim(padded, first_row, group_size, 0)
        delay_block = lax.dynamic_slice_in_dim(delay_rows, first_row, group_size, 0)
        phase_block = lax.dynamic_slice_in_dim(phase_rows, first_row, group_size, 0)
        starts = delay_block + offset_base
        gathered = row_slices(pulses_block, starts, out_cells).astype(jnp.float32)
        cosine = jnp.cos(phase_block)[:, :, None]
        sine_part = jnp.sin(phase_block)[:, :, None]
        real_part = gathered[:, :, 0] * cosine - gathered[:, :, 1] * sine_part
        imag_part = gathered[:, :, 0] * sine_part + gathered[:, :, 1] * cosine
        return (summed + jnp.stack([jnp.sum(real_part, axis=0), jnp.sum(imag_part, axis=0)]), None)

    summed, unused = lax.scan(
        accumulate,
        jnp.zeros((2, beam_count, out_cells), jnp.float32),
        jnp.arange(block_count, dtype=jnp.int32),
    )
    return summed * inside_mask(first_cell, out_cells) * (1.0 / math.sqrt(pulses))


def tap_weights(tap_values):
    weights = SPREAD + 1.0 - jnp.abs(tap_values).astype(jnp.float32)
    return weights / jnp.sum(weights)


def merge_side(
    source,
    beam_rows,
    offsets,
    phase_zero,
    phase_slope,
    weights,
    tap_values,
    offset_base,
    out_cells,
    first_cell,
):
    picked = jnp.take(source, beam_rows, axis=1)
    span = out_cells + 2 * SPREAD
    starts = offsets + offset_base - SPREAD
    windows = jax.vmap(
        lambda beam_data, start: lax.dynamic_slice_in_dim(beam_data, start, span, 1),
        in_axes=(1, 0),
        out_axes=1,
    )(picked, starts)
    summed = jnp.zeros((2, beam_rows.shape[0], out_cells), jnp.float32)
    for tap_index in range(tap_values.shape[0]):
        tap_start = tap_values[tap_index] + SPREAD
        summed = summed + weights[tap_index] * lax.dynamic_slice_in_dim(
            windows, tap_start, out_cells, 2
        )
    positions = jnp.arange(out_cells, dtype=jnp.int32)
    global_cells = (first_cell + positions).astype(jnp.float32)
    angle_grid = (
        phase_zero[:, None] + 2.0 * math.pi / R * phase_slope[:, None] * global_cells[None, :]
    )
    cosine = jnp.cos(angle_grid)
    sine_part = jnp.sin(angle_grid)
    return jnp.stack(
        [summed[0] * cosine - summed[1] * sine_part, summed[0] * sine_part + summed[1] * cosine]
    )


def pick_sides(table, level_index, side_bit):
    half_rows = lax.dynamic_index_in_dim(table[level_index], side_bit, 0, keepdims=False)
    own_rows = lax.dynamic_index_in_dim(half_rows, side_bit, 0, keepdims=False)
    other_rows = lax.dynamic_index_in_dim(half_rows, 1 - side_bit, 0, keepdims=False)
    return (own_rows, other_rows)


def local(
    raw_echoes,
    matched,
    delays,
    pulse_phase,
    beam_map,
    range_shift,
    phase_base,
    phase_rate,
    tap_offsets,
):
    pulses = raw_echoes.shape[0]
    hop_bins = raw_echoes.shape[3]
    local_cells = raw_echoes.shape[1] * hop_bins
    forward_exact, inverse_exact = tables(BLOCK)
    forward = forward_exact.astype(jnp.bfloat16)
    inverse_kept = kept_columns(inverse_exact.astype(jnp.bfloat16), BLOCK)
    tail = shifted(raw_echoes[:, -1], "rng", 1)
    compressed = compress(raw_echoes, tail, matched, forward_exact, forward, inverse_kept)
    compressed = jnp.transpose(compressed, (0, 2, 1, 3)).reshape(pulses, 2, local_cells)
    first_cell = lax.axis_index("rng") * local_cells
    rim_cells = SHIFT + SPREAD
    margin_cells = LEVELS * rim_cells
    padded = padded_2(compressed, (("rng", 2),), SHIFT + margin_cells)
    polar_image = project(
        padded,
        delays,
        pulse_phase,
        SHIFT,
        local_cells + 2 * margin_cells,
        first_cell - margin_cells,
    )
    pulse_index = lax.axis_index("pulse")
    for level_index in range(LEVELS):
        side_bit = pulse_index // 2**level_index % 2
        own_beams, other_beams = pick_sides(beam_map, level_index, side_bit)
        own_offsets, other_offsets = pick_sides(range_shift, level_index, side_bit)
        own_zero, other_zero = pick_sides(phase_base, level_index, side_bit)
        own_slope, other_slope = pick_sides(phase_rate, level_index, side_bit)
        tap_values = tap_offsets[level_index]
        weights = tap_weights(tap_values)
        received = from_partner(polar_image, "pulse", level_index)
        own_source = polar_image
        out_margin = max(margin_cells - rim_cells * (level_index + 1), 0)
        out_cells = local_cells + 2 * out_margin
        start_cell = first_cell - out_margin
        own_side = merge_side(
            own_source,
            own_beams,
            own_offsets,
            own_zero,
            own_slope,
            weights,
            tap_values,
            rim_cells,
            out_cells,
            start_cell,
        )
        other_side = merge_side(
            received,
            other_beams,
            other_offsets,
            other_zero,
            other_slope,
            weights,
            tap_values,
            rim_cells,
            out_cells,
            start_cell,
        )
        polar_image = (own_side + other_side) * SQRT_HALF * inside_mask(start_cell, out_cells)
    return polar_image


def solution(mesh):
    in_specs = (
        P(("grp", "pulse"), "rng", None, None),
        P(),
        P(("grp", "pulse"), None),
        P(("grp", "pulse"), None),
        P(),
        P(),
        P(),
        P(),
        P(),
    )
    out_specs = P(None, ("grp", "pulse"), "rng")
    return jax.shard_map(local, mesh=mesh, in_specs=in_specs, out_specs=out_specs, check_vma=False)
```

profile of v0, /device:TPU:0, one launch (start us, length us, event | category | flops | bytes accessed | tf_op | source)
XLA Modules:
  0.0 847.7 jit_solution(4714250410205099282)
XLA Ops:
  17.8 2.5 broadcast_divide_fusion.3
  49.2 2.2 concatenate.78
  51.4 271.4 %while.33 = (s32[]{:T(128)}, f32[2,16,8416]{2,1,0:T(8,128)S(1)}, s32[2]{0:T(128)S(1)}, bf16[8,2,8464]{2,1,0:T(2,128)(2,1)}, s32[8,16]{1,0:T(8,128)}, /*index=5*/...) while((s32[]{:T(128)}, f32[2,16,8416]{2,1,0:T(8,128)S(1)}, ...), condition=%wide.region_7.8_spmd.clone, body=%wide.region_4.7_spmd.clone.sunk | while | flops 4848073 | bytes 17581828 | solution.py:128
  54.5 128.3 %while.34 = (s32[]{:T(128)}, bf16[4,2,8464]{2,1,0:T(2,128)(2,1)S(1)}, s32[64,3]{0,1:T(4,128)S(1)}, bf16[64,2,8416]{2,1,0:T(2,128)(2,1)S(1)}, s32[]{:T(128)}) while((s32[]{:T(128)}, bf16[4,2,8464]{2,1,0:T(2,128)(2,1)S(1)}, s32[64,3]{0,1:T(4,128)S(1)}, bf16[64,2,8416]{2,1,0:T(2,128)(2,1)S(1)}, s32[]{:T(128)}) %tuple.302), condition=%wide.while_cond, body=%wide.while_body.sunk | while | flops 2 | bytes 67709 | solution.py:104
  182.8 3.0 fusion.178
  190.2 128.3 %while.34 = (s32[]{:T(128)}, bf16[4,2,8464]{2,1,0:T(2,128)(2,1)S(1)}, s32[64,3]{0,1:T(4,128)S(1)}, bf16[64,2,8416]{2,1,0:T(2,128)(2,1)S(1)}, s32[]{:T(128)}) while((s32[]{:T(128)}, bf16[4,2,8464]{2,1,0:T(2,128)(2,1)S(1)}, s32[64,3]{0,1:T(4,128)S(1)}, bf16[64,2,8416]{2,1,0:T(2,128)(2,1)S(1)}, s32[]{:T(128)}) %tuple.302), condition=%wide.while_cond, body=%wide.while_body.sunk | while | flops 2 | bytes 67709 | solution.py:104
  318.4 3.0 fusion.178
  325.1 2.1 copy.77
  330.3 54.2 %while.24 = (s32[]{:T(128)}, f32[16,2,8416]{2,1,0:T(2,128)S(1)}, s32[16,3]{0,1:T(4,128)S(1)}, f32[16,2,8368]{2,0,1:T(8,128)S(1)}, s32[]{:T(128)}, /*index=5*/s32[]{:T(128)}) while((s32[]{:T(128)}, f32[16,2,8416]{2,1,0:T(2,128)S(1)}, s32[16,3]{0,1:T(4,128)S(1)}, f32[16,2,8368]{2,0,1:T(8,128)S(1)}, s32[]{:T(128)}, /*index=5*/s32[]{:T(128)}) %tuple.334), condition=%wide.while_cond.1, body=%wide.while_body.1.sunk | while | flops 2 | bytes 401797 | solution.py:157
  384.5 3.6 add_bitcast_fusion.1
  388.1 2.1 copy.82
  394.3 67.4 %while.25 = (s32[]{:T(128)}, f32[16,2,8416]{2,1,0:T(2,128)}, s32[16,3]{0,1:T(4,128)S(1)}, f32[16,2,8368]{2,0,1:T(8,128)S(1)}, s32[]{:T(128)}, /*index=5*/s32[]{:T(128)}) while((s32[]{:T(128)}, f32[16,2,8416]{2,1,0:T(2,128)}, s32[16,3]{0,1:T(4,128)S(1)}, f32[16,2,8368]{2,0,1:T(8,128)S(1)}, s32[]{:T(128)}, /*index=5*/s32[]{:T(128)}) %tuple.333), condition=%wide.while_cond.2, body=%wide.while_body.2.sunk | while | flops 2 | bytes 401797 | solution.py:157
  394.9 2.3 constant_dynamic-slice_fusion.71
  399.1 2.3 constant_dynamic-slice_fusion.71
  403.3 2.3 constant_dynamic-slice_fusion.71
  407.6 2.3 constant_dynamic-slice_fusion.71
  411.8 2.3 constant_dynamic-slice_fusion.71
  416.0 2.3 constant_dynamic-slice_fusion.71
  420.2 2.3 constant_dynamic-slice_fusion.71
  424.4 2.3 constant_dynamic-slice_fusion.71
  428.6 2.3 constant_dynamic-slice_fusion.71
  432.8 2.3 constant_dynamic-slice_fusion.71
  437.1 2.3 constant_dynamic-slice_fusion.71
  441.3 2.3 constant_dynamic-slice_fusion.71
  445.5 2.3 constant_dynamic-slice_fusion.71
  449.7 2.3 constant_dynamic-slice_fusion.71
  453.9 2.3 constant_dynamic-slice_fusion.71
  458.1 2.3 constant_dynamic-slice_fusion.71
  461.7 3.6 add_bitcast_fusion
  465.4 4.2 multiply_subtract_fusion
  469.7 2.5 collective-permute-start.4
  476.2 53.1 %while.26 = (s32[]{:T(128)}, f32[16,2,8360]{2,1,0:T(2,128)S(1)}, s32[16,3]{0,1:T(4,128)S(1)}, f32[16,2,8312]{2,0,1:T(8,128)S(1)}, s32[]{:T(128)}, /*index=5*/s32[]{:T(128)}) while((s32[]{:T(128)}, f32[16,2,8360]{2,1,0:T(2,128)S(1)}, s32[16,3]{0,1:T(4,128)S(1)}, f32[16,2,8312]{2,0,1:T(8,128)S(1)}, s32[]{:T(128)}, /*index=5*/s32[]{:T(128)}) %tuple.332), condition=%wide.while_cond.3, body=%wide.while_body.3.sunk | while | flops 2 | bytes 399109 | solution.py:157
  529.3 3.6 add_bitcast_fusion.5
  532.9 2.1 copy.92
  537.5 50.3 %while.27 = (s32[]{:T(128)}, f32[16,2,8360]{2,1,0:T(2,128)S(1)}, s32[16,3]{0,1:T(4,128)S(1)}, f32[16,2,8312]{2,0,1:T(8,128)S(1)}, s32[]{:T(128)}, /*index=5*/s32[]{:T(128)}) while((s32[]{:T(128)}, f32[16,2,8360]{2,1,0:T(2,128)S(1)}, s32[16,3]{0,1:T(4,128)S(1)}, f32[16,2,8312]{2,0,1:T(8,128)S(1)}, s32[]{:T(128)}, /*index=5*/s32[]{:T(128)}) %tuple.314), condition=%wide.while_cond.4, body=%wide.while_body.4.sunk | while | flops 2 | bytes 399109 | solution.py:157
  587.8 3.6 add_bitcast_fusion.4
  591.5 4.1 multiply_subtract_fusion.4
  600.4 50.2 %while.28 = (s32[]{:T(128)}, f32[16,2,8304]{2,1,0:T(2,128)S(1)}, s32[16,3]{0,1:T(4,128)S(1)}, f32[16,2,8256]{2,0,1:T(8,128)S(1)}, s32[]{:T(128)}, /*index=5*/s32[]{:T(128)}) while((s32[]{:T(128)}, f32[16,2,8304]{2,1,0:T(2,128)S(1)}, s32[16,3]{0,1:T(4,128)S(1)}, f32[16,2,8256]{2,0,1:T(8,128)S(1)}, s32[]{:T(128)}, /*index=5*/s32[]{:T(128)}) %tuple.323), condition=%wide.while_cond.5, body=%wide.while_body.5.sunk | while | flops 2 | bytes 396421 | solution.py:157
  650.7 3.8 add_bitcast_fusion.3
  658.7 52.3 %while.29 = (s32[]{:T(128)}, f32[16,2,8304]{2,1,0:T(2,128)S(1)}, s32[16,3]{0,1:T(4,128)S(1)}, f32[16,2,8256]{2,0,1:T(8,128)S(1)}, s32[]{:T(128)}, /*index=5*/s32[]{:T(128)}) while((s32[]{:T(128)}, f32[16,2,8304]{2,1,0:T(2,128)S(1)}, s32[16,3]{0,1:T(4,128)S(1)}, f32[16,2,8256]{2,0,1:T(8,128)S(1)}, s32[]{:T(128)}, /*index=5*/s32[]{:T(128)}) %tuple.320), condition=%wide.while_cond.6, body=%wide.while_body.6.sunk | while | flops 2 | bytes 396421 | solution.py:157
  711.0 3.8 add_bitcast_fusion.2
  714.8 4.1 multiply_subtract_fusion.2
  719.1 2.7 collective-permute-start.6
  724.8 53.4 %while.30 = (s32[]{:T(128)}, f32[16,2,8248]{2,1,0:T(2,128)S(1)}, s32[16,3]{0,1:T(4,128)S(1)}, f32[16,2,8200]{2,0,1:T(8,128)S(1)}, s32[]{:T(128)}, /*index=5*/s32[]{:T(128)}) while((s32[]{:T(128)}, f32[16,2,8248]{2,1,0:T(2,128)S(1)}, s32[16,3]{0,1:T(4,128)S(1)}, f32[16,2,8200]{2,0,1:T(8,128)S(1)}, s32[]{:T(128)}, /*index=5*/s32[]{:T(128)}) %tuple.329), condition=%wide.while_cond.7, body=%wide.while_body.7.sunk | while | flops 2 | bytes 393733 | solution.py:157
  778.2 3.6 add_bitcast_fusion.7
  786.0 52.3 %while.31 = (s32[]{:T(128)}, f32[16,2,8248]{2,1,0:T(2,128)S(1)}, s32[16,3]{0,1:T(4,128)S(1)}, f32[16,2,8200]{2,0,1:T(8,128)S(1)}, s32[]{:T(128)}, /*index=5*/s32[]{:T(128)}) while((s32[]{:T(128)}, f32[16,2,8248]{2,1,0:T(2,128)S(1)}, s32[16,3]{0,1:T(4,128)S(1)}, f32[16,2,8200]{2,0,1:T(8,128)S(1)}, s32[]{:T(128)}, /*index=5*/s32[]{:T(128)}) %tuple.326), condition=%wide.while_cond.8, body=%wide.while_body.8.sunk | while | flops 2 | bytes 393733 | solution.py:157
  838.4 3.6 add_bitcast_fusion.6
  842.1 4.0 multiply_subtract_fusion.6
  (1220 shorter events, 710.7 us)
Async XLA Ops:
  0.0 6.0 copy-start.5
  0.0 9.9 %copy-start.38 = (f32[2,128]{1,0:T(2,128)S(1)}, f32[2,128]{1,0:T(2,128)}, u32[]{:S(2)}) copy-start(f32[2,128]{1,0:T(2,128)} %param.20) | copy-start | bytes 3076
  0.7 36.0 %collective-permute-start = (bf16[8,2,128]{2,1,0:T(2,128)(2,1)S(1)}, bf16[8,2,128]{2,1,0:T(2,128)(2,1)S(1)}, u32[]{:S(2)}, u32[]{:S(2)}) collective-permute-start(bf16[8,2,128]{2,1,0:T(2,128)(2,1)S(1)} %slice_bitcast_fusion), channel_id=1, source_target_pairs={} | collective-permute-start | bytes 12296 | tf_op jit(solution)/shard_map/ppermute | solution.py:21
  6.0 4.5 copy-start.10
  6.0 5.8 copy-start.11
  7.4 4.4 copy-start.12
  7.4 4.4 copy-start.13
  9.9 26.8 %copy-start = (bf16[8,64,2,128]{3,2,1,0:T(2,128)(2,1)S(1)}, bf16[8,64,2,128]{3,2,1,0:T(2,128)(2,1)}, u32[]{:S(2)}) copy-start(bf16[8,64,2,128]{3,2,1,0:T(2,128)(2,1)} %param.19) | copy-start | bytes 786436
  9.9 26.8 %slice-start = ((bf16[8,64,2,128]{3,2,1,0:T(2,128)(2,1)}), bf16[8,63,2,128]{3,2,1,0:T(2,128)(2,1)S(1)}, s32[]{:S(2)}) async-start(bf16[8,64,2,128]{3,2,1,0:T(2,128)(2,1)} %param.19), calls=%async_computation | async-start | bytes 516096 | tf_op jit(solution)/shard_map/slice | solution.py:73
  38.7 10.5 %collective-permute-start.1 = (bf16[8,2,136]{2,1,0:T(2,128)(2,1)S(1)}, bf16[8,2,136]{2,1,0:T(2,128)(2,1)S(1)}, u32[]{:S(2)}, u32[]{:S(2)}) collective-permute-start(bf16[8,2,136]{2,1,0:T(2,128)(2,1)S(1)} %get-tuple-element.360), channel_id=1, source_target_pairs={} | collective-permute-start | bytes 13064 | tf_op jit(solution)/shard_map/ppermute | solution.py:29
  39.4 9.8 %collective-permute-start.2 = (bf16[8,2,136]{2,1,0:T(2,128)(2,1)S(1)}, bf16[8,2,136]{2,1,0:T(2,128)(2,1)S(1)}, u32[]{:S(2)}, u32[]{:S(2)}) collective-permute-start(bf16[8,2,136]{2,1,0:T(2,128)(2,1)S(1)} %get-tuple-element.359), channel_id=1, source_target_pairs={} | collective-permute-start | bytes 13064 | tf_op jit(solution)/shard_map/ppermute | solution.py:32
  51.4 1.2 copy-start.39
  182.7 3.0 copy-start.9
  187.1 1.2 copy-start.39
  318.4 3.0 copy-start.9
  324.6 63.5 %collective-permute-start.3 = (f32[2,16,8416]{2,1,0:T(8,128)}, f32[2,16,8416]{2,1,0:T(8,128)}, u32[]{:S(2)}, u32[]{:S(2)}) collective-permute-start(f32[2,16,8416]{2,1,0:T(8,128)} %multiply_multiply_fusion), channel_id=1, source_target_pairs={{0,1},{1,0},{2,3},{3,2},{4,5},{5,4},{6,7},{7,6},{8,9},{9,8},{10,11... | collective-permute-start | bytes 3231752 | tf_op jit(solution)/shard_map/ppermute | solution.py:44
  327.2 1.9 copy-start.33
  390.2 1.9 copy-start.32
  461.7 3.7 copy-start.22
  461.7 3.7 copy-start.23
  461.7 3.7 copy-start.24
  461.7 3.7 copy-start.25
  465.4 4.2 copy-start.2
  469.7 63.2 %collective-permute-start.4 = (f32[2,16,8360]{2,1,0:T(8,128)S(1)}, f32[2,16,8360]{2,1,0:T(8,128)}, u32[]{:S(2)}, u32[]{:S(2)}) collective-permute-start(f32[2,16,8360]{2,1,0:T(8,128)S(1)} %fusion.6), channel_id=1, source_target_pairs={{0,2},{2,0},{1,3},{3,1},{4,6},{6,4},{5,7},{7,5},{8,10},{10,8},{9,1... | collective-permute-start | bytes 3210248 | tf_op jit(solution)/shard_map/ppermute | solution.py:44
  473.1 1.9 copy-start.31
  475.5 0.7 copy-start.6
  535.0 1.9 copy-start.30
  587.8 3.7 copy-start.18
  587.8 3.7 copy-start.19
  587.8 3.7 copy-start.20
  587.8 3.7 copy-start.21
  591.5 4.1 copy-start.1
  595.8 58.7 %collective-permute-start.5 = (f32[2,16,8304]{2,1,0:T(8,128)S(1)}, f32[2,16,8304]{2,1,0:T(8,128)}, u32[]{:S(2)}, u32[]{:S(2)}) collective-permute-start(f32[2,16,8304]{2,1,0:T(8,128)S(1)} %fusion.7), channel_id=1, source_target_pairs={{0,4},{4,0},{1,5},{5,1},{2,6},{6,2},{3,7},{7,3},{8,12},{12,8},{9,1... | collective-permute-start | bytes 3188744 | tf_op jit(solution)/shard_map/ppermute | solution.py:44
  598.0 1.8 copy-start.29
  656.2 1.8 copy-start.28
  711.0 3.8 copy-start.14
  711.0 3.8 copy-start.15
  711.0 3.8 copy-start.16
  711.0 3.8 copy-start.17
  719.1 62.7 %collective-permute-start.6 = (f32[2,16,8248]{2,1,0:T(8,128)S(1)}, f32[2,16,8248]{2,1,0:T(8,128)}, u32[]{:S(2)}, u32[]{:S(2)}) collective-permute-start(f32[2,16,8248]{2,1,0:T(8,128)S(1)} %fusion.8), channel_id=1, source_target_pairs={{0,8},{8,0},{1,9},{9,1},{2,10},{10,2},{3,11},{11,3},{4,12},{12,4},... | collective-permute-start | bytes 3167240 | tf_op jit(solution)/shard_map/ppermute | solution.py:44
  722.3 1.8 copy-start.27
  783.6 1.8 copy-start.26
  838.3 3.7 copy-start.4
  838.3 3.7 copy-start.34
  838.3 3.7 copy-start.35
  838.3 3.7 copy-start.36
  838.4 3.7 copy-start.37
  842.1 4.1 copy-start.3
  (4 other events, 2.6 us)
where the time goes:
time: 860 us; the launch traced here: 848 us
  local copies, waits for them, and re-layouts  725 us (84%)
  other arithmetic  79.5 us (9%)
  between operations  22 us (3%)
  loops' own time  9.77 us (1%)
  starting transfers between devices  9.49 us (1%)
    gather x1024, local copies, waits for them, and re-layouts  681 us
    add x8, other arithmetic, merge_side(): summed + weights[tap_index] * lax.dynamic_slice_in_dim(windows, tap_start...  29.3 us
  transfers between devices with their start and end apart: 7, of which 0 were waited for; matrix products, arithmetic and copies ran while one was open for 31% of the time, Pallas kernels for 0%

commit v1 on v0

--- a/solution.py
+++ b/solution.py
@@ -1,8 +1,11 @@
+import functools
 import math
 
 import jax
 import jax.numpy as jnp
 from jax import lax
+from jax.experimental import pallas as pl
+from jax.experimental.pallas import tpu as pltpu
 from jax.sharding import PartitionSpec as P
 
 R = 8192
@@ -257,6 +260,313 @@
     return polar_image
 
 
+LANES = 128
+EDGE = 32
+
+
+def flip_parts(value, lane):
+    return jnp.where(
+        lane % 2 == 0, -pltpu.roll(value, LANES - 1, 1), pltpu.roll(value, 1, 1)
+    )
+
+
+def from_previous(value, lane):
+    return jnp.where(lane < 2, 0.0, pltpu.roll(value, 2, 1))
+
+
+def from_next(value, lane):
+    return jnp.where(lane >= LANES - 2, 0.0, pltpu.roll(value, LANES - 2, 1))
+
+
+def store_extended(target, slot, value):
+    rows = value.shape[0]
+    lane = lax.broadcasted_iota(jnp.int32, (EDGE, LANES), 1)
+    target[slot, EDGE : EDGE + rows, :] = value
+    target[slot, 0:EDGE, :] = from_previous(value[rows - EDGE :], lane)
+    target[slot, EDGE + rows :, :] = from_next(value[:EDGE], lane)
+
+
+def kernel(
+    pulses,
+    beams,
+    span,
+    echo_ref,
+    matched_ref,
+    delay_ref,
+    trig_ref,
+    map_ref,
+    shift_ref,
+    base_ref,
+    rate_ref,
+    tap_ref,
+    out_ref,
+    taps_hold,
+    pulse_ext,
+    image,
+    other,
+    filt,
+    table,
+    partial,
+    outgoing,
+    incoming,
+    turned,
+    send_sem,
+    recv_sem,
+):
+    levels = tap_ref.shape[0]
+    tap_count = tap_ref.shape[1]
+    rows = echo_ref.shape[1]
+    me = lax.axis_index("pulse")
+    partners = []
+    bits = []
+    for level in range(levels):
+        bit = me // 2**level % 2
+        bits.append(bit)
+        partners.append(me + (1 - 2 * bit) * 2**level)
+
+    barrier = pltpu.get_barrier_semaphore()
+    for partner in partners:
+        pl.semaphore_signal(
+            barrier, inc=1, device_id={"pulse": partner}, device_id_type=pl.DeviceIdType.MESH
+        )
+
+    lane = lax.broadcasted_iota(jnp.int32, (rows, LANES), 1)
+    row = lax.broadcasted_iota(jnp.int32, (rows, LANES), 0)
+
+    for part in range(2):
+        spread_taps = jnp.broadcast_to(matched_ref[part : part + 1, :], (rows, LANES))
+        circulant = jnp.transpose(pltpu.roll(spread_taps, 0, 1, stride=1, stride_axis=0))
+        for side in range(2):
+            kept = jnp.where((row >= lane) == (side == 0), circulant, 0.0)
+            high = kept.astype(jnp.bfloat16)
+            low = (kept - high.astype(jnp.float32)).astype(jnp.bfloat16)
+            place = (part * 2 + side) * rows
+            taps_hold[0, place : place + rows, :] = high
+            taps_hold[1, place : place + rows, :] = low
+
+    def compress_pulse(pulse, carry):
+        first = pl.multiple_of(pulse * LANES, LANES)
+        data = echo_ref[pl.ds(first, LANES), :]
+
+        def times(part, side):
+            place = (part * 2 + side) * rows
+            dims = (((1,), (1,)), ((), ()))
+            return lax.dot_general(
+                taps_hold[0, place : place + rows, :], data, dims, preferred_element_type=jnp.float32
+            ) + lax.dot_general(
+                taps_hold[1, place : place + rows, :], data, dims, preferred_element_type=jnp.float32
+            )
+
+        real_taps = times(0, 0) + from_previous(times(0, 1), lane)
+        imag_taps = times(1, 0) + from_previous(times(1, 1), lane)
+        store_extended(pulse_ext, pulse, real_taps + flip_parts(imag_taps, lane))
+        return carry
+
+    lax.fori_loop(0, pulses, compress_pulse, 0)
+
+    def project_beam(beam, carry):
+        cos_sum = jnp.zeros((rows, LANES), jnp.float32)
+        sin_sum = jnp.zeros((rows, LANES), jnp.float32)
+        for pulse in range(pulses):
+            slab = pulse_ext[pulse, pl.ds(EDGE + delay_ref[pulse, beam], rows), :]
+            cos_sum += trig_ref[0, pulse, beam] * slab
+            sin_sum += trig_ref[1, pulse, beam] * slab
+        value = cos_sum + flip_parts(sin_sum, lane)
+        store_extended(image, beam, value)
+        outgoing[0, beam] = value.astype(jnp.bfloat16)
+        return carry
+
+    lax.fori_loop(0, beams, project_beam, 0)
+    pl.semaphore_wait(barrier, levels)
+
+    small_lane = lax.broadcasted_iota(jnp.int32, (8, LANES), 1)
+    small_row = lax.broadcasted_iota(jnp.int32, (8, LANES), 0)
+    cells = (small_lane // 2 * rows + small_row).astype(jnp.float32)
+    filt_rows = filt.shape[2]
+    copies = []
+    for level in range(levels):
+        bit = bits[level]
+        own_first = bit * (beams - span)
+        their_first = (1 - bit) * (beams - span)
+        copy = pltpu.make_async_remote_copy(
+            src_ref=outgoing.at[level, pl.ds(their_first, span)],
+            dst_ref=incoming.at[level],
+            send_sem=send_sem.at[level],
+            recv_sem=recv_sem.at[level],
+            device_id={"pulse": partners[level]},
+            device_id_type=pl.DeviceIdType.MESH,
+        )
+        copy.start()
+        copies.append(copy)
+
+        raw_weights = [
+            jnp.full(
+                (8, LANES), SPREAD + 1 - jnp.abs(tap_ref[level, tap]), jnp.int32
+            ).astype(jnp.float32)
+            for tap in range(tap_count)
+        ]
+        total = raw_weights[0]
+        for weight in raw_weights[1:]:
+            total = total + weight
+        weights = [
+            jnp.tile(weight * SQRT_HALF / total, (filt_rows // 8, 1)) for weight in raw_weights
+        ]
+
+        def fill_table(index, carry, level=level, bit=bit):
+            side = index // beams
+            beam = index % beams
+            zero = base_ref[level, bit, side, beam]
+            slope = rate_ref[level, bit, side, beam] * (2.0 * math.pi / R)
+            angle = zero + slope * cells
+            step = jnp.full((8, LANES), slope * 8.0, jnp.float32)
+            cosine, sine = jnp.cos(angle), jnp.sin(angle)
+            step_cos, step_sin = jnp.cos(step), jnp.sin(step)
+            stack = [(cosine, sine)]
+            while len(stack) * 8 < rows:
+                stack = stack + [
+                    (c * step_cos - s * step_sin, s * step_cos + c * step_sin) for c, s in stack
+                ]
+                step_cos, step_sin = (
+                    step_cos * step_cos - step_sin * step_sin,
+                    2.0 * step_cos * step_sin,
+                )
+            for place, (c, s) in enumerate(stack):
+                table[0, index, place * 8 : place * 8 + 8, :] = c
+                table[1, index, place * 8 : place * 8 + 8, :] = s
+            return carry
+
+        lax.fori_loop(0, 2 * beams, fill_table, 0)
+
+        def filter_rows(source, slot, level=level, weights=weights):
+            summed = None
+            for tap in range(tap_count):
+                start = EDGE - SHIFT + tap_ref[level, tap]
+                term = weights[tap] * source[slot, pl.ds(start, filt_rows), :]
+                summed = term if summed is None else summed + term
+            return summed
+
+        def filter_own(index, carry, own_first=own_first, filter_rows=filter_rows):
+            filt[0, index] = filter_rows(image, own_first + index)
+            return carry
+
+        lax.fori_loop(0, span, filter_own, 0)
+
+        def slab_of(which, side, beam, level=level, bit=bit, own_first=own_first):
+            source = jnp.clip(map_ref[level, bit, side, beam] - own_first, 0, span - 1)
+            start = SHIFT + shift_ref[level, bit, side, beam]
+            return filt[which, source, pl.ds(start, rows), :]
+
+        def merge_own(beam, carry, bit=bit, slab_of=slab_of):
+            slab = slab_of(0, bit, beam)
+            index = bit * beams + beam
+            partial[0, beam] = table[0, index] * slab
+            partial[1, beam] = table[1, index] * slab
+            return carry
+
+        lax.fori_loop(0, beams, merge_own, 0)
+        copy.wait_recv()
+
+        def filter_other(index, carry, level=level, filter_rows=filter_rows):
+            store_extended(other, 0, incoming[level, index].astype(jnp.float32))
+            filt[1, index] = filter_rows(other, 0)
+            return carry
+
+        lax.fori_loop(0, span, filter_other, 0)
+
+        def merge_other(beam, carry, level=level, bit=bit, slab_of=slab_of):
+            slab = slab_of(1, 1 - bit, beam)
+            index = (1 - bit) * beams + beam
+            cos_sum = partial[0, beam] + table[0, index] * slab
+            sin_sum = partial[1, beam] + table[1, index] * slab
+            value = cos_sum + flip_parts(sin_sum, lane)
+            if level + 1 < levels:
+                store_extended(image, beam, value)
+                outgoing[level + 1, beam] = value.astype(jnp.bfloat16)
+            else:
+                first = pl.multiple_of(beam * LANES, LANES)
+                turned[pl.ds(first, LANES), :] = jnp.transpose(value)
+            return carry
+
+        lax.fori_loop(0, beams, merge_other, 0)
+
+    def put_block(block, carry):
+        column = pl.multiple_of(block * rows, rows)
+        for part in range(2):
+            for group in range(beams // 8):
+                start = group * 8 * LANES + 2 * block + part
+                out_ref[part, group * 8 : group * 8 + 8, pl.ds(column, rows)] = turned[
+                    pl.ds(start, 8, stride=LANES), :
+                ]
+        return carry
+
+    lax.fori_loop(0, LANES // 2, put_block, 0)
+    for copy in copies:
+        copy.wait_send()
+
+
+def local_fused(
+    raw_echoes,
+    matched,
+    delays,
+    pulse_phase,
+    beam_map,
+    range_shift,
+    phase_base,
+    phase_rate,
+    tap_offsets,
+):
+    pulses, blocks, parts, hop_bins = raw_echoes.shape
+    beams = delays.shape[1]
+    levels = tap_offsets.shape[0]
+    span = beams // 2 + 1
+    echoes = raw_echoes.reshape(pulses * blocks * parts, hop_bins)
+    trig = jnp.stack([jnp.cos(pulse_phase), jnp.sin(pulse_phase)]) * (1.0 / math.sqrt(pulses))
+    vmem = pl.BlockSpec(memory_space=pltpu.VMEM)
+    smem = pl.BlockSpec(memory_space=pltpu.SMEM)
+    extended = hop_bins + 2 * EDGE
+    return pl.pallas_call(
+        functools.partial(kernel, pulses, beams, span),
+        out_shape=jax.ShapeDtypeStruct((parts, beams, blocks * hop_bins), jnp.float32),
+        in_specs=[vmem, vmem] + [smem] * 7,
+        out_specs=vmem,
+        scratch_shapes=[
+            pltpu.VMEM((2, 4 * hop_bins, LANES), jnp.bfloat16),
+            pltpu.VMEM((pulses, extended, LANES), jnp.float32),
+            pltpu.VMEM((beams, extended, LANES), jnp.float32),
+            pltpu.VMEM((1, extended, LANES), jnp.float32),
+            pltpu.VMEM((2, span, hop_bins + 2 * SHIFT, LANES), jnp.float32),
+            pltpu.VMEM((2, 2 * beams, hop_bins, LANES), jnp.float32),
+            pltpu.VMEM((2, beams, hop_bins, LANES), jnp.float32),
+            pltpu.VMEM((levels, beams, hop_bins, LANES), jnp.bfloat16),
+            pltpu.VMEM((levels, span, hop_bins, LANES), jnp.bfloat16),
+            pltpu.VMEM((beams * LANES, hop_bins), jnp.float32),
+            pltpu.SemaphoreType.DMA((levels,)),
+            pltpu.SemaphoreType.DMA((levels,)),
+        ],
+        compiler_params=pltpu.CompilerParams(
+            collective_id=0, has_side_effects=True, vmem_limit_bytes=48 * 2**20
+        ),
+    )(
+        echoes,
+        matched,
+        delays,
+        trig,
+        beam_map,
+        range_shift,
+        phase_base,
+        phase_rate,
+        tap_offsets,
+    )
+
+
+def local_any(raw_echoes, *rest):
+    pulses, blocks, parts, hop_bins = raw_echoes.shape
+    paired = lax.axis_size("pulse") % 2**LEVELS == 0
+    if lax.axis_size("rng") == 1 and blocks * parts == LANES and hop_bins == LANES and paired:
+        return local_fused(raw_echoes, *rest)
+    return local(raw_echoes, *rest)
+
+
 def solution(mesh):
     in_specs = (
         P(("grp", "pulse"), "rng", None, None),
@@ -270,4 +580,4 @@
         P(),
     )
     out_specs = P(None, ("grp", "pulse"), "rng")
-    return jax.shard_map(local, mesh=mesh, in_specs=in_specs, out_specs=out_specs, check_vma=False)
+    return jax.shard_map(local_any, mesh=mesh, in_specs=in_specs, out_specs=out_specs, check_vma=False)

time: 860 us -> 65.1 us (0.08); the launches traced: 848 us -> 64.8 us
  local copies, waits for them, and re-layouts: 725 us -> 4.72 us
  other arithmetic: 79.5 us -> 0.01 us
  Pallas kernels: 0 us -> 60 us
  between operations: 22 us -> 0.06 us
  loops' own time: 9.77 us -> 0 us
  starting transfers between devices: 9.49 us -> 0 us
    gather x1034 -> x0, local copies, waits for them, and re-layouts: 696 us -> none
    pallas_call x0 -> x1, Pallas kernels: none -> 60 us  [local_fused(): pl.pallas_call(functools.partial(kernel, pulses, beams, span), out_shape=...]
    add x14 -> x0, other arithmetic: 32.3 us -> none  [the longest x8 29.3 us: merge_side(): summed + weights[tap_index] * lax.dynamic_slice_in_dim(windows, tap_start...]
    sub x4 -> x0, other arithmetic: 16.4 us -> none  [merge_side(): summed[0] * cosine - summed[1] * sine_part]
    another operation x11 -> x0, loops' own time: 9.77 us -> none  [the longest x8 6.05 us: merge_side(): lax.dynamic_slice_in_dim(beam_data, start, span, 1)]
    ppermute x7 -> x0, starting transfers between devices: 9.49 us -> none  [the longest x4 7.33 us: from_partner(): return lax.ppermute(block, axis, route)]
  transfers between devices with their start and end apart: 7 -> 0, of which waited for: 0 -> 0; matrix products, arithmetic and copies ran while one was open for 31% -> 0% of each run, Pallas kernels for 0% -> 0%
where the time goes in v1:
time: 65.1 us; the launch traced here: 64.8 us
  Pallas kernels  60 us (92%)
  local copies, waits for them, and re-layouts  4.72 us (7%)
    pallas_call x1, Pallas kernels, local_fused(): pl.pallas_call(functools.partial(kernel, pulses, beams, span), out_shape=...  60 us
    unnamed x17, local copies, waits for them, and re-layouts  3.97 us

profile of v1, /device:TPU:0, one launch (start us, length us, event | category | flops | bytes accessed | tf_op | source)
XLA Modules:
  0.0 64.8 jit_solution(5877156732478045959)
XLA Ops:
  0.0 0.0 copy-start.4
  0.0 0.0 copy-start.3
  0.0 0.8 %cosine_bitcast_fusion = (f32[1,8,16]{2,1,0:T(8,128)S(1)}, f32[1,8,16]{2,1,0:T(8,128)S(1)}) fusion(f32[8,16]{1,0:T(8,128)} %param.12), kind=kLoop, calls=%fused_computation.2 | loop fusion | bytes 1536 | tf_op jit(solution)/shard_map/stack | solution.py:523
  0.8 0.0 copy-start.7
  0.8 0.0 copy-start.1
  0.8 0.0 copy-start.2
  0.8 0.0 copy-done.4
  0.8 0.0 copy-done.3
  0.8 0.6 copy-done.7
  1.4 0.0 copy-done.1
  1.5 0.0 copy-done.2
  1.5 0.0 copy-start
  1.5 0.9 %copy-done = bf16[8,64,2,128]{3,2,1,0:T(2,128)(2,1)S(1)} copy-done((bf16[8,64,2,128]{3,2,1,0:T(2,128)(2,1)S(1)}, bf16[8,64,2,128]{3,2,1,0:T(2,128)(2,1)}, u32[]{:S(2)}) %copy-start) | copy-done | bytes 262168
  2.4 0.0 copy-start.5
  2.4 0.7 %copy-done.5 = s32[8,16]{1,0:T(8,128)S(1)} copy-done((s32[8,16]{1,0:T(8,128)S(1)}, s32[8,16]{1,0:T(8,128)}, u32[]{:S(2)}) %copy-start.5) | copy-done | bytes 536
  3.1 0.0 copy-start.6
  3.1 0.7 %copy-done.6 = s32[4,4]{1,0:T(4,128)S(1)} copy-done((s32[4,4]{1,0:T(4,128)S(1)}, s32[4,4]{1,0:T(4,128)}, u32[]{:S(2)}) %copy-start.6) | copy-done | bytes 88
  3.8 60.0 %shard_map.91 = f32[2,16,8192]{2,1,0:T(8,128)S(1)} custom-call(bf16[1024,128]{1,0:T(8,128)(2,1)S(1)} %bitcast.5, f32[2,128]{1,0:T(2,128)S(1)} %copy-done.7, s32[8,16]{1,0:T(8,128)S(1)} %copy-done.5, f32[2,8,16]{2,1,0:T(8,128)S(1)} %maximum_multiply_fusion.trig_ref, s32[4,2,2,16]{3,2,1,0:T(2,128)S(1)} %copy-done.1, s32[4,2,2,16]{3,2,1,0:T(2,128)S(1)} %copy-done.2, ...), custom_call_target="tpu_custom_call" | custom-call | tf_op jit(solution)/shard_map/pallas_call | solution.py:527
  63.9 1.0 %copy.11 = f32[2,16,8192]{2,1,0:T(8,128)} copy(f32[2,16,8192]{2,1,0:T(8,128)S(1)} %shard_map.91) | data formatting | bytes 2097152
  (1 shorter events, 0.0 us)
Async XLA Ops:
  0.0 0.8 %copy-start.4 = (f32[4,2,2,16]{3,2,1,0:T(2,128)S(1)}, f32[4,2,2,16]{3,2,1,0:T(2,128)}, u32[]{:S(2)}) copy-start(f32[4,2,2,16]{3,2,1,0:T(2,128)} %rate_ref.1) | copy-start | bytes 3076
  0.0 0.8 %copy-start.3 = (f32[4,2,2,16]{3,2,1,0:T(2,128)S(1)}, f32[4,2,2,16]{3,2,1,0:T(2,128)}, u32[]{:S(2)}) copy-start(f32[4,2,2,16]{3,2,1,0:T(2,128)} %base_ref.1) | copy-start | bytes 3076
  0.8 0.7 %copy-start.7 = (f32[2,128]{1,0:T(2,128)S(1)}, f32[2,128]{1,0:T(2,128)}, u32[]{:S(2)}) copy-start(f32[2,128]{1,0:T(2,128)} %matched_ref.1) | copy-start | bytes 3076
  0.8 0.7 %copy-start.1 = (s32[4,2,2,16]{3,2,1,0:T(2,128)S(1)}, s32[4,2,2,16]{3,2,1,0:T(2,128)}, u32[]{:S(2)}) copy-start(s32[4,2,2,16]{3,2,1,0:T(2,128)} %map_ref.1) | copy-start | bytes 3076
  0.8 0.7 %copy-start.2 = (s32[4,2,2,16]{3,2,1,0:T(2,128)S(1)}, s32[4,2,2,16]{3,2,1,0:T(2,128)}, u32[]{:S(2)}) copy-start(s32[4,2,2,16]{3,2,1,0:T(2,128)} %shift_ref.1) | copy-start | bytes 3076
  1.5 0.9 %copy-start = (bf16[8,64,2,128]{3,2,1,0:T(2,128)(2,1)S(1)}, bf16[8,64,2,128]{3,2,1,0:T(2,128)(2,1)}, u32[]{:S(2)}) copy-start(bf16[8,64,2,128]{3,2,1,0:T(2,128)(2,1)} %param.9) | copy-start | bytes 786436
  2.4 0.7 %copy-start.5 = (s32[8,16]{1,0:T(8,128)S(1)}, s32[8,16]{1,0:T(8,128)}, u32[]{:S(2)}) copy-start(s32[8,16]{1,0:T(8,128)} %delay_ref.1) | copy-start | bytes 1540
  3.1 0.7 %copy-start.6 = (s32[4,4]{1,0:T(4,128)S(1)}, s32[4,4]{1,0:T(4,128)}, u32[]{:S(2)}) copy-start(s32[4,4]{1,0:T(4,128)} %tap_ref.1) | copy-start | bytes 196

commit v2 on v1

--- a/solution.py
+++ b/solution.py
@@ -286,6 +286,28 @@
     target[slot, EDGE + rows :, :] = from_next(value[:EDGE], lane)
 
 
+def early_plan(beams, span):
+    needs = [0] * span
+    for low in (0, beams - span):
+        for turn in (0, 2):
+            for half in (0, 1):
+                for position in range(span):
+                    beam = low + (position + turn) % span
+                    start = 2 if low else 0
+                    for step in (-1, 0, 1):
+                        child = min(max(beam // 2 + step + half * (beams // 2), 0), beams - 1)
+                        place = (child - half * (beams - span) - start) % span
+                        needs[position] = max(needs[position], place + 1)
+    plan = []
+    for position in range(span):
+        need = max(needs[: position + 1])
+        if plan and plan[-1][0] == need:
+            plan[-1] = (need, position + 1)
+        else:
+            plan.append((need, position + 1))
+    return plan
+
+
 def kernel(
     pulses,
     beams,
@@ -306,7 +328,6 @@
     other,
     filt,
     table,
-    partial,
     outgoing,
     incoming,
     turned,
@@ -324,6 +345,8 @@
         bits.append(bit)
         partners.append(me + (1 - 2 * bit) * 2**level)
 
+    turns = [2 * (1 - bits[level + 1]) for level in range(levels - 1)] + [0]
+
     barrier = pltpu.get_barrier_semaphore()
     for partner in partners:
         pl.semaphore_signal(
@@ -364,40 +387,55 @@
 
     lax.fori_loop(0, pulses, compress_pulse, 0)
 
-    def project_beam(beam, carry):
+    def beam_at(level, position):
+        first = (1 - bits[level]) * (beams - span)
+        early = first + lax.rem(position + turns[level], span)
+        late = bits[level] * span + position - span
+        return early, late
+
+    def transfer(level, position):
+        return pltpu.make_async_remote_copy(
+            src_ref=outgoing.at[level, position],
+            dst_ref=incoming.at[level, position],
+            send_sem=send_sem.at[level, position],
+            recv_sem=recv_sem.at[level, position],
+            device_id={"pulse": partners[level]},
+            device_id_type=pl.DeviceIdType.MESH,
+        )
+
+    def project_beam(beam):
         cos_sum = jnp.zeros((rows, LANES), jnp.float32)
         sin_sum = jnp.zeros((rows, LANES), jnp.float32)
         for pulse in range(pulses):
             slab = pulse_ext[pulse, pl.ds(EDGE + delay_ref[pulse, beam], rows), :]
             cos_sum += trig_ref[0, pulse, beam] * slab
             sin_sum += trig_ref[1, pulse, beam] * slab
-        value = cos_sum + flip_parts(sin_sum, lane)
-        store_extended(image, beam, value)
-        outgoing[0, beam] = value.astype(jnp.bfloat16)
-        return carry
-
-    lax.fori_loop(0, beams, project_beam, 0)
+        return cos_sum + flip_parts(sin_sum, lane)
+
+    def produce(level, make, low, high):
+        def step(position, carry):
+            early, late = beam_at(level, position)
+            beam = early if high <= span else late
+            value = make(beam)
+            if high <= span:
+                outgoing[level, position] = value.astype(jnp.bfloat16)
+                transfer(level, position).start()
+            store_extended(image, beam, value)
+            return carry
+
+        lax.fori_loop(low, high, step, 0)
+
     pl.semaphore_wait(barrier, levels)
+    produce(0, project_beam, 0, span)
+    produce(0, project_beam, span, beams)
 
     small_lane = lax.broadcasted_iota(jnp.int32, (8, LANES), 1)
     small_row = lax.broadcasted_iota(jnp.int32, (8, LANES), 0)
     cells = (small_lane // 2 * rows + small_row).astype(jnp.float32)
     filt_rows = filt.shape[2]
-    copies = []
     for level in range(levels):
         bit = bits[level]
         own_first = bit * (beams - span)
-        their_first = (1 - bit) * (beams - span)
-        copy = pltpu.make_async_remote_copy(
-            src_ref=outgoing.at[level, pl.ds(their_first, span)],
-            dst_ref=incoming.at[level],
-            send_sem=send_sem.at[level],
-            recv_sem=recv_sem.at[level],
-            device_id={"pulse": partners[level]},
-            device_id_type=pl.DeviceIdType.MESH,
-        )
-        copy.start()
-        copies.append(copy)
 
         raw_weights = [
             jnp.full(
@@ -412,9 +450,8 @@
             jnp.tile(weight * SQRT_HALF / total, (filt_rows // 8, 1)) for weight in raw_weights
         ]
 
-        def fill_table(index, carry, level=level, bit=bit):
-            side = index // beams
-            beam = index % beams
+        def fill_one(side, beam, level=level, bit=bit):
+            index = side * beams + beam
             zero = base_ref[level, bit, side, beam]
             slope = rate_ref[level, bit, side, beam] * (2.0 * math.pi / R)
             angle = zero + slope * cells
@@ -433,9 +470,11 @@
             for place, (c, s) in enumerate(stack):
                 table[0, index, place * 8 : place * 8 + 8, :] = c
                 table[1, index, place * 8 : place * 8 + 8, :] = s
+
+        def fill_table(beam, carry, fill_one=fill_one):
+            fill_one(0, beam)
+            fill_one(1, beam)
             return carry
-
-        lax.fori_loop(0, 2 * beams, fill_table, 0)
 
         def filter_rows(source, slot, level=level, weights=weights):
             summed = None
@@ -449,45 +488,50 @@
             filt[0, index] = filter_rows(image, own_first + index)
             return carry
 
-        lax.fori_loop(0, span, filter_own, 0)
+        def filter_other(position, carry, level=level, filter_rows=filter_rows):
+            transfer(level, position).wait_recv()
+            place = lax.rem(position + turns[level], span)
+            store_extended(other, 0, incoming[level, position].astype(jnp.float32))
+            filt[1, place] = filter_rows(other, 0)
+            return carry
 
         def slab_of(which, side, beam, level=level, bit=bit, own_first=own_first):
             source = jnp.clip(map_ref[level, bit, side, beam] - own_first, 0, span - 1)
             start = SHIFT + shift_ref[level, bit, side, beam]
             return filt[which, source, pl.ds(start, rows), :]
 
-        def merge_own(beam, carry, bit=bit, slab_of=slab_of):
-            slab = slab_of(0, bit, beam)
-            index = bit * beams + beam
-            partial[0, beam] = table[0, index] * slab
-            partial[1, beam] = table[1, index] * slab
+        def merge(beam, bit=bit, slab_of=slab_of):
+            own_slab, own_index = slab_of(0, bit, beam), bit * beams + beam
+            other_slab, other_index = slab_of(1, 1 - bit, beam), (1 - bit) * beams + beam
+            cos_sum = table[0, own_index] * own_slab + table[0, other_index] * other_slab
+            sin_sum = table[1, own_index] * own_slab + table[1, other_index] * other_slab
+            return cos_sum + flip_parts(sin_sum, lane)
+
+        def finish(beam, carry, merge=merge):
+            first = pl.multiple_of(beam * LANES, LANES)
+            turned[pl.ds(first, LANES), :] = jnp.transpose(merge(beam))
             return carry
 
-        lax.fori_loop(0, beams, merge_own, 0)
-        copy.wait_recv()
-
-        def filter_other(index, carry, level=level, filter_rows=filter_rows):
-            store_extended(other, 0, incoming[level, index].astype(jnp.float32))
-            filt[1, index] = filter_rows(other, 0)
-            return carry
-
-        lax.fori_loop(0, span, filter_other, 0)
-
-        def merge_other(beam, carry, level=level, bit=bit, slab_of=slab_of):
-            slab = slab_of(1, 1 - bit, beam)
-            index = (1 - bit) * beams + beam
-            cos_sum = partial[0, beam] + table[0, index] * slab
-            sin_sum = partial[1, beam] + table[1, index] * slab
-            value = cos_sum + flip_parts(sin_sum, lane)
-            if level + 1 < levels:
-                store_extended(image, beam, value)
-                outgoing[level + 1, beam] = value.astype(jnp.bfloat16)
-            else:
-                first = pl.multiple_of(beam * LANES, LANES)
-                turned[pl.ds(first, LANES), :] = jnp.transpose(value)
-            return carry
-
-        lax.fori_loop(0, beams, merge_other, 0)
+        lax.fori_loop(0, span, filter_own, 0)
+        lax.fori_loop(0, beams, fill_table, 0)
+        arrived = 0
+        if level + 1 < levels:
+            made = 0
+            for count, until in early_plan(beams, span):
+                lax.fori_loop(arrived, count, filter_other, 0)
+                produce(level + 1, merge, made, until)
+                arrived, made = count, until
+            lax.fori_loop(arrived, span, filter_other, 0)
+            produce(level + 1, merge, span, beams)
+        else:
+            lax.fori_loop(0, 2, filter_other, 0)
+
+            def child_then_pair(position, carry, filter_other=filter_other, finish=finish):
+                filter_other(position, 0)
+                return lax.fori_loop(2 * position - 4, 2 * position - 2, finish, carry)
+
+            lax.fori_loop(2, span, child_then_pair, 0)
+            lax.fori_loop(2 * span - 4, beams, finish, 0)
 
     def put_block(block, carry):
         column = pl.multiple_of(block * rows, rows)
@@ -500,8 +544,13 @@
         return carry
 
     lax.fori_loop(0, LANES // 2, put_block, 0)
-    for copy in copies:
-        copy.wait_send()
+
+    def drain(position, carry):
+        for level in range(levels):
+            transfer(level, position).wait_send()
+        return carry
+
+    lax.fori_loop(0, span, drain, 0)
 
 
 def local_fused(
@@ -536,12 +585,11 @@
             pltpu.VMEM((1, extended, LANES), jnp.float32),
             pltpu.VMEM((2, span, hop_bins + 2 * SHIFT, LANES), jnp.float32),
             pltpu.VMEM((2, 2 * beams, hop_bins, LANES), jnp.float32),
-            pltpu.VMEM((2, beams, hop_bins, LANES), jnp.float32),
-            pltpu.VMEM((levels, beams, hop_bins, LANES), jnp.bfloat16),
+            pltpu.VMEM((levels, span, hop_bins, LANES), jnp.bfloat16),
             pltpu.VMEM((levels, span, hop_bins, LANES), jnp.bfloat16),
             pltpu.VMEM((beams * LANES, hop_bins), jnp.float32),
-            pltpu.SemaphoreType.DMA((levels,)),
-            pltpu.SemaphoreType.DMA((levels,)),
+            pltpu.SemaphoreType.DMA((levels, span)),
+            pltpu.SemaphoreType.DMA((levels, span)),
         ],
         compiler_params=pltpu.CompilerParams(
             collective_id=0, has_side_effects=True, vmem_limit_bytes=48 * 2**20

time: 65.1 us -> 48.7 us (0.75)
  Pallas kernels: 60 us -> 43.6 us
    pallas_call x1, Pallas kernels: 60 us -> 43.6 us  [local_fused(): pl.pallas_call(functools.partial(kernel, pulses, beams, span), out_shape=...]
where the time goes in v2:
time: 48.7 us; the launch traced here: 48.4 us
  Pallas kernels  43.6 us (90%)
  local copies, waits for them, and re-layouts  4.72 us (10%)
    pallas_call x1, Pallas kernels, local_fused(): pl.pallas_call(functools.partial(kernel, pulses, beams, span), out_shape=...  43.6 us
    unnamed x17, local copies, waits for them, and re-layouts  3.97 us

profile of v2, /device:TPU:0, one launch (start us, length us, event | category | flops | bytes accessed | tf_op | source)
XLA Modules:
  0.0 48.4 jit_solution(1619308973527778866)
XLA Ops:
  0.0 0.0 copy-start.4
  0.0 0.0 copy-start.3
  0.0 0.8 %cosine_bitcast_fusion = (f32[1,8,16]{2,1,0:T(8,128)S(1)}, f32[1,8,16]{2,1,0:T(8,128)S(1)}) fusion(f32[8,16]{1,0:T(8,128)} %param.12), kind=kLoop, calls=%fused_computation.2 | loop fusion | bytes 1536 | tf_op jit(solution)/shard_map/stack | solution.py:572
  0.8 0.0 copy-start.7
  0.8 0.0 copy-start.1
  0.8 0.0 copy-start.2
  0.8 0.0 copy-done.4
  0.8 0.0 copy-done.3
  0.8 0.6 %copy-done.7 = f32[2,128]{1,0:T(2,128)S(1)} copy-done((f32[2,128]{1,0:T(2,128)S(1)}, f32[2,128]{1,0:T(2,128)}, u32[]{:S(2)}) %copy-start.7) | copy-done | bytes 1048
  1.4 0.0 copy-done.1
  1.5 0.0 copy-done.2
  1.5 0.0 copy-start
  1.5 0.9 %copy-done = bf16[8,64,2,128]{3,2,1,0:T(2,128)(2,1)S(1)} copy-done((bf16[8,64,2,128]{3,2,1,0:T(2,128)(2,1)S(1)}, bf16[8,64,2,128]{3,2,1,0:T(2,128)(2,1)}, u32[]{:S(2)}) %copy-start) | copy-done | bytes 262168
  2.4 0.0 copy-start.5
  2.4 0.7 %copy-done.5 = s32[8,16]{1,0:T(8,128)S(1)} copy-done((s32[8,16]{1,0:T(8,128)S(1)}, s32[8,16]{1,0:T(8,128)}, u32[]{:S(2)}) %copy-start.5) | copy-done | bytes 536
  3.1 0.0 copy-start.6
  3.1 0.7 %copy-done.6 = s32[4,4]{1,0:T(4,128)S(1)} copy-done((s32[4,4]{1,0:T(4,128)S(1)}, s32[4,4]{1,0:T(4,128)}, u32[]{:S(2)}) %copy-start.6) | copy-done | bytes 88
  3.8 43.6 %shard_map.91 = f32[2,16,8192]{2,1,0:T(8,128)S(1)} custom-call(bf16[1024,128]{1,0:T(8,128)(2,1)S(1)} %bitcast.5, f32[2,128]{1,0:T(2,128)S(1)} %copy-done.7, s32[8,16]{1,0:T(8,128)S(1)} %copy-done.5, f32[2,8,16]{2,1,0:T(8,128)S(1)} %maximum_multiply_fusion.trig_ref, s32[4,2,2,16]{3,2,1,0:T(2,128)S(1)} %copy-done.1, s32[4,2,2,16]{3,2,1,0:T(2,128)S(1)} %copy-done.2, ...), custom_call_target="tpu_custom_call" | custom-call | tf_op jit(solution)/shard_map/pallas_call | solution.py:576
  47.4 1.0 %copy.11 = f32[2,16,8192]{2,1,0:T(8,128)} copy(f32[2,16,8192]{2,1,0:T(8,128)S(1)} %shard_map.91) | data formatting | bytes 2097152
  (1 shorter events, 0.0 us)
Async XLA Ops:
  0.0 0.8 %copy-start.4 = (f32[4,2,2,16]{3,2,1,0:T(2,128)S(1)}, f32[4,2,2,16]{3,2,1,0:T(2,128)}, u32[]{:S(2)}) copy-start(f32[4,2,2,16]{3,2,1,0:T(2,128)} %rate_ref.1) | copy-start | bytes 3076
  0.0 0.8 %copy-start.3 = (f32[4,2,2,16]{3,2,1,0:T(2,128)S(1)}, f32[4,2,2,16]{3,2,1,0:T(2,128)}, u32[]{:S(2)}) copy-start(f32[4,2,2,16]{3,2,1,0:T(2,128)} %base_ref.1) | copy-start | bytes 3076
  0.8 0.7 %copy-start.7 = (f32[2,128]{1,0:T(2,128)S(1)}, f32[2,128]{1,0:T(2,128)}, u32[]{:S(2)}) copy-start(f32[2,128]{1,0:T(2,128)} %matched_ref.1) | copy-start | bytes 3076
  0.8 0.7 %copy-start.1 = (s32[4,2,2,16]{3,2,1,0:T(2,128)S(1)}, s32[4,2,2,16]{3,2,1,0:T(2,128)}, u32[]{:S(2)}) copy-start(s32[4,2,2,16]{3,2,1,0:T(2,128)} %map_ref.1) | copy-start | bytes 3076
  0.8 0.7 %copy-start.2 = (s32[4,2,2,16]{3,2,1,0:T(2,128)S(1)}, s32[4,2,2,16]{3,2,1,0:T(2,128)}, u32[]{:S(2)}) copy-start(s32[4,2,2,16]{3,2,1,0:T(2,128)} %shift_ref.1) | copy-start | bytes 3076
  1.5 0.9 %copy-start = (bf16[8,64,2,128]{3,2,1,0:T(2,128)(2,1)S(1)}, bf16[8,64,2,128]{3,2,1,0:T(2,128)(2,1)}, u32[]{:S(2)}) copy-start(bf16[8,64,2,128]{3,2,1,0:T(2,128)(2,1)} %param.9) | copy-start | bytes 786436
  2.4 0.7 %copy-start.5 = (s32[8,16]{1,0:T(8,128)S(1)}, s32[8,16]{1,0:T(8,128)}, u32[]{:S(2)}) copy-start(s32[8,16]{1,0:T(8,128)} %delay_ref.1) | copy-start | bytes 1540
  3.1 0.7 %copy-start.6 = (s32[4,4]{1,0:T(4,128)S(1)}, s32[4,4]{1,0:T(4,128)}, u32[]{:S(2)}) copy-start(s32[4,4]{1,0:T(4,128)} %tap_ref.1) | copy-start | bytes 196

commit v3 on v2

--- a/solution.py
+++ b/solution.py
@@ -286,6 +286,20 @@
     target[slot, EDGE + rows :, :] = from_next(value[:EDGE], lane)
 
 
+def sin_cos(turns):
+    half_turns = jnp.floor(2.0 * turns + 0.5)
+    angle = (turns - 0.5 * half_turns) * (2.0 * math.pi)
+    sign = 1.0 - 2.0 * (half_turns - 2.0 * jnp.floor(0.5 * half_turns))
+    square = angle * angle
+    sine = jnp.full_like(angle, -1.0 / math.factorial(11))
+    cosine = jnp.full_like(angle, 1.0 / math.factorial(12))
+    for power in (9, 7, 5, 3, 1):
+        sine = sine * square + (-1.0) ** (power // 2) / math.factorial(power)
+    for power in (10, 8, 6, 4, 2, 0):
+        cosine = cosine * square + (-1.0) ** (power // 2) / math.factorial(power)
+    return sign * angle * sine, sign * cosine
+
+
 def early_plan(beams, span):
     needs = [0] * span
     for low in (0, beams - span):
@@ -312,16 +326,25 @@
     pulses,
     beams,
     span,
-    echo_ref,
-    matched_ref,
-    delay_ref,
+    *refs,
+):
+    sources, (out_ref,), held, work = refs[:9], refs[9:10], refs[10:20], refs[20:]
+    (
+        echo_ref,
+        matched_ref,
+        phase_ref,
+        delay_ref,
+        map_ref,
+        shift_ref,
+        base_ref,
+        rate_ref,
+        tap_ref,
+        load_sem,
+    ) = held
+    (
+    trig_hold,
     trig_ref,
-    map_ref,
-    shift_ref,
-    base_ref,
-    rate_ref,
-    tap_ref,
-    out_ref,
+    trig_sem,
     taps_hold,
     pulse_ext,
     image,
@@ -333,7 +356,13 @@
     turned,
     send_sem,
     recv_sem,
-):
+    ) = work
+    loads = [
+        pltpu.make_async_copy(source, target, load_sem.at[place])
+        for place, (source, target) in enumerate(zip(sources, held))
+    ]
+    for place in (2, 1, 0, 3, 4, 5, 6, 7, 8):
+        loads[place].start()
     levels = tap_ref.shape[0]
     tap_count = tap_ref.shape[1]
     rows = echo_ref.shape[1]
@@ -356,6 +385,14 @@
     lane = lax.broadcasted_iota(jnp.int32, (rows, LANES), 1)
     row = lax.broadcasted_iota(jnp.int32, (rows, LANES), 0)
 
+    loads[2].wait()
+    sine, cosine = sin_cos(phase_ref[...] * (0.5 / math.pi))
+    trig_hold[0] = cosine * (1.0 / math.sqrt(pulses))
+    trig_hold[1] = sine * (1.0 / math.sqrt(pulses))
+    to_scalars = pltpu.make_async_copy(trig_hold, trig_ref, trig_sem)
+    to_scalars.start()
+    loads[1].wait()
+
     for part in range(2):
         spread_taps = jnp.broadcast_to(matched_ref[part : part + 1, :], (rows, LANES))
         circulant = jnp.transpose(pltpu.roll(spread_taps, 0, 1, stride=1, stride_axis=0))
@@ -385,7 +422,11 @@
         store_extended(pulse_ext, pulse, real_taps + flip_parts(imag_taps, lane))
         return carry
 
+    loads[0].wait()
     lax.fori_loop(0, pulses, compress_pulse, 0)
+    for load in loads[3:]:
+        load.wait()
+    to_scalars.wait()
 
     def beam_at(level, position):
         first = (1 - bits[level]) * (beams - span)
@@ -424,6 +465,18 @@
             return carry
 
         lax.fori_loop(low, high, step, 0)
+
+    def put_group(group):
+        def put_block(block, carry):
+            column = pl.multiple_of(block * rows, rows)
+            for part in range(2):
+                start = group * 8 * LANES + 2 * block + part
+                out_ref[part, group * 8 : group * 8 + 8, pl.ds(column, rows)] = turned[
+                    pl.ds(start, 8, stride=LANES), :
+                ]
+            return carry
+
+        lax.fori_loop(0, LANES // 2, put_block, 0, unroll=4)
 
     pl.semaphore_wait(barrier, levels)
     produce(0, project_beam, 0, span)
@@ -452,12 +505,10 @@
 
         def fill_one(side, beam, level=level, bit=bit):
             index = side * beams + beam
-            zero = base_ref[level, bit, side, beam]
-            slope = rate_ref[level, bit, side, beam] * (2.0 * math.pi / R)
-            angle = zero + slope * cells
-            step = jnp.full((8, LANES), slope * 8.0, jnp.float32)
-            cosine, sine = jnp.cos(angle), jnp.sin(angle)
-            step_cos, step_sin = jnp.cos(step), jnp.sin(step)
+            zero = base_ref[level, bit, side, beam] * (0.5 / math.pi)
+            slope = rate_ref[level, bit, side, beam] * (1.0 / R)
+            sine, cosine = sin_cos(zero + slope * cells)
+            step_sin, step_cos = sin_cos(jnp.full((8, LANES), slope * 8.0, jnp.float32))
             stack = [(cosine, sine)]
             while len(stack) * 8 < rows:
                 stack = stack + [
@@ -530,20 +581,13 @@
                 filter_other(position, 0)
                 return lax.fori_loop(2 * position - 4, 2 * position - 2, finish, carry)
 
-            lax.fori_loop(2, span, child_then_pair, 0)
-            lax.fori_loop(2 * span - 4, beams, finish, 0)
-
-    def put_block(block, carry):
-        column = pl.multiple_of(block * rows, rows)
-        for part in range(2):
+            done = 2
             for group in range(beams // 8):
-                start = group * 8 * LANES + 2 * block + part
-                out_ref[part, group * 8 : group * 8 + 8, pl.ds(column, rows)] = turned[
-                    pl.ds(start, 8, stride=LANES), :
-                ]
-        return carry
-
-    lax.fori_loop(0, LANES // 2, put_block, 0)
+                until = min(4 * group + 6, span)
+                lax.fori_loop(done, until, child_then_pair, 0)
+                lax.fori_loop(2 * until - 4, 8 * group + 8, finish, 0)
+                put_group(group)
+                done = until
 
     def drain(position, carry):
         for level in range(levels):
@@ -569,16 +613,34 @@
     levels = tap_offsets.shape[0]
     span = beams // 2 + 1
     echoes = raw_echoes.reshape(pulses * blocks * parts, hop_bins)
-    trig = jnp.stack([jnp.cos(pulse_phase), jnp.sin(pulse_phase)]) * (1.0 / math.sqrt(pulses))
     vmem = pl.BlockSpec(memory_space=pltpu.VMEM)
-    smem = pl.BlockSpec(memory_space=pltpu.SMEM)
+    hbm = pl.BlockSpec(memory_space=pltpu.HBM)
+    operands = (
+        echoes,
+        matched,
+        pulse_phase,
+        delays,
+        beam_map,
+        range_shift,
+        phase_base,
+        phase_rate,
+        tap_offsets,
+    )
     extended = hop_bins + 2 * EDGE
     return pl.pallas_call(
         functools.partial(kernel, pulses, beams, span),
         out_shape=jax.ShapeDtypeStruct((parts, beams, blocks * hop_bins), jnp.float32),
-        in_specs=[vmem, vmem] + [smem] * 7,
+        in_specs=[hbm] * len(operands),
         out_specs=vmem,
         scratch_shapes=[
+            (pltpu.VMEM if place < 3 else pltpu.SMEM)(operand.shape, operand.dtype)
+            for place, operand in enumerate(operands)
+        ]
+        + [
+            pltpu.SemaphoreType.DMA((len(operands),)),
+            pltpu.VMEM((2,) + pulse_phase.shape, jnp.float32),
+            pltpu.SMEM((2,) + pulse_phase.shape, jnp.float32),
+            pltpu.SemaphoreType.DMA,
             pltpu.VMEM((2, 4 * hop_bins, LANES), jnp.bfloat16),
             pltpu.VMEM((pulses, extended, LANES), jnp.float32),
             pltpu.VMEM((beams, extended, LANES), jnp.float32),
@@ -592,19 +654,9 @@
             pltpu.SemaphoreType.DMA((levels, span)),
         ],
         compiler_params=pltpu.CompilerParams(
-            collective_id=0, has_side_effects=True, vmem_limit_bytes=48 * 2**20
+            collective_id=0, has_side_effects=True, vmem_limit_bytes=64946176
         ),
-    )(
-        echoes,
-        matched,
-        delays,
-        trig,
-        beam_map,
-        range_shift,
-        phase_base,
-        phase_rate,
-        tap_offsets,
-    )
+    )(*operands)
 
 
 def local_any(raw_echoes, *rest):

time: 48.7 us -> 45.3 us (0.930)
  local copies, waits for them, and re-layouts: 4.72 us -> 2.26 us
  Pallas kernels: 43.6 us -> 42.9 us
    unnamed x17 -> x1, local copies, waits for them, and re-layouts: 3.97 us -> 2.26 us
    another operation x1 -> x0, local copies, waits for them, and re-layouts: 0.75 us -> none  [local_fused(): jnp.stack([jnp.cos(pulse_phase), jnp.sin(pulse_phase)])]
    pallas_call x1, Pallas kernels: 43.6 us -> 42.9 us  [local_fused(): pl.pallas_call(functools.partial(kernel, pulses, beams, span), out_shape=...]
where the time goes in v3:
time: 45.3 us; the launch traced here: 45.2 us
  Pallas kernels  42.9 us (95%)
  local copies, waits for them, and re-layouts  2.26 us (5%)
    pallas_call x1, Pallas kernels, local_fused(): pl.pallas_call(functools.partial(kernel, pulses, beams, span), out_shape=...  42.9 us
    unnamed x1, local copies, waits for them, and re-layouts  2.26 us

profile of v3, /device:TPU:0, one launch (start us, length us, event | category | flops | bytes accessed | tf_op | source)
XLA Modules:
  0.0 45.2 jit_solution(13364956763552736274)
XLA Ops:
  0.0 42.9 %shard_map.91 = f32[2,16,8192]{2,1,0:T(8,128)} custom-call(bf16[1024,128]{1,0:T(8,128)(2,1)} %bitcast.1, f32[2,128]{1,0:T(2,128)} %refs_1_.1, f32[8,16]{1,0:T(8,128)} %refs_2_.1, s32[8,16]{1,0:T(8,128)} %refs_3_.1, s32[4,2,2,16]{3,2,1,0:T(2,128)} %refs_4_.1, s32[4,2,2,16]{3,2,1,0:T(2,128)} %refs_5_.1, f32[4,2,2,16]{3,2,1,0:T(2,128)} %refs_6_.1, ...), custom_call_target="tpu_custom_call" | custom-call | tf_op jit(solution)/shard_map/pallas_call | solution.py:630
  42.9 2.3 %copy.11 = f32[2,16,8192]{2,1,0:T(8,128)} copy(f32[2,16,8192]{2,1,0:T(8,128)} %shard_map.91) | data formatting | bytes 2097152

commit v4 on v3

--- a/solution.py
+++ b/solution.py
@@ -464,7 +464,7 @@
             store_extended(image, beam, value)
             return carry
 
-        lax.fori_loop(low, high, step, 0)
+        lax.fori_loop(low, high, step, 0, unroll=min(high - low, 3))
 
     def put_group(group):
         def put_block(block, carry):
@@ -563,8 +563,8 @@
             turned[pl.ds(first, LANES), :] = jnp.transpose(merge(beam))
             return carry
 
-        lax.fori_loop(0, span, filter_own, 0)
-        lax.fori_loop(0, beams, fill_table, 0)
+        lax.fori_loop(0, span, filter_own, 0, unroll=3)
+        lax.fori_loop(0, beams, fill_table, 0, unroll=2)
         arrived = 0
         if level + 1 < levels:
             made = 0
@@ -654,9 +654,9 @@
             pltpu.SemaphoreType.DMA((levels, span)),
         ],
         compiler_params=pltpu.CompilerParams(
-            collective_id=0, has_side_effects=True, vmem_limit_bytes=64946176
+            collective_id=0, has_side_effects=True, vmem_limit_bytes=48 * 2**20
         ),
-    )(*operands)
+    )(*[pltpu.with_memory_space_constraint(operand, pltpu.HBM) for operand in operands])
 
 
 def local_any(raw_echoes, *rest):

time: 45.3 us -> 41.8 us (0.923)
  Pallas kernels: 42.9 us -> 40.6 us
  local copies, waits for them, and re-layouts: 2.26 us -> 0.97 us
    pallas_call x1, Pallas kernels: 42.9 us -> 40.6 us  [local_fused(): pl.pallas_call(functools.partial(kernel, pulses, beams, span), out_shape=...]
    unnamed x1, local copies, waits for them, and re-layouts: 2.26 us -> 0.97 us
where the time goes in v4:
time: 41.8 us; the launch traced here: 41.6 us
  Pallas kernels  40.6 us (97%)
  local copies, waits for them, and re-layouts  0.97 us (2%)
    pallas_call x1, Pallas kernels, local_fused(): pl.pallas_call(functools.partial(kernel, pulses, beams, span), out_shape=...  40.6 us
    unnamed x1, local copies, waits for them, and re-layouts  0.97 us

profile of v4, /device:TPU:0, one launch (start us, length us, event | category | flops | bytes accessed | tf_op | source)
XLA Modules:
  0.0 41.6 jit_solution(14056708092494649477)
XLA Ops:
  0.0 40.6 %shard_map.91 = f32[2,16,8192]{2,1,0:T(8,128)S(1)} custom-call(bf16[1024,128]{1,0:T(8,128)(2,1)} %bitcast.1, f32[2,128]{1,0:T(2,128)} %refs_1_.1, f32[8,16]{1,0:T(8,128)} %refs_2_.1, s32[8,16]{1,0:T(8,128)} %refs_3_.1, s32[4,2,2,16]{3,2,1,0:T(2,128)} %refs_4_.1, s32[4,2,2,16]{3,2,1,0:T(2,128)} %refs_5_.1, f32[4,2,2,16]{3,2,1,0:T(2,128)} %refs_6_.1, ...), custom_call_target="tpu_custom_call" | custom-call | tf_op jit(solution)/shard_map/pallas_call | solution.py:630
  40.6 1.0 %copy.11 = f32[2,16,8192]{2,1,0:T(8,128)} copy(f32[2,16,8192]{2,1,0:T(8,128)S(1)} %shard_map.91) | data formatting | bytes 2097152

commit v5 on v4

--- a/solution.py
+++ b/solution.py
@@ -423,7 +423,7 @@
         return carry
 
     loads[0].wait()
-    lax.fori_loop(0, pulses, compress_pulse, 0)
+    lax.fori_loop(0, pulses, compress_pulse, 0, unroll=2)
     for load in loads[3:]:
         load.wait()
     to_scalars.wait()
@@ -464,7 +464,7 @@
             store_extended(image, beam, value)
             return carry
 
-        lax.fori_loop(low, high, step, 0, unroll=min(high - low, 3))
+        lax.fori_loop(low, high, step, 0, unroll=True)
 
     def put_group(group):
         def put_block(block, carry):
@@ -563,13 +563,13 @@
             turned[pl.ds(first, LANES), :] = jnp.transpose(merge(beam))
             return carry
 
-        lax.fori_loop(0, span, filter_own, 0, unroll=3)
-        lax.fori_loop(0, beams, fill_table, 0, unroll=2)
+        lax.fori_loop(0, span, filter_own, 0, unroll=True)
+        lax.fori_loop(0, beams, fill_table, 0, unroll=4)
         arrived = 0
         if level + 1 < levels:
             made = 0
             for count, until in early_plan(beams, span):
-                lax.fori_loop(arrived, count, filter_other, 0)
+                lax.fori_loop(arrived, count, filter_other, 0, unroll=True)
                 produce(level + 1, merge, made, until)
                 arrived, made = count, until
             lax.fori_loop(arrived, span, filter_other, 0)
@@ -579,13 +579,13 @@
 
             def child_then_pair(position, carry, filter_other=filter_other, finish=finish):
                 filter_other(position, 0)
-                return lax.fori_loop(2 * position - 4, 2 * position - 2, finish, carry)
+                return finish(2 * position - 3, finish(2 * position - 4, carry))
 
             done = 2
             for group in range(beams // 8):
                 until = min(4 * group + 6, span)
                 lax.fori_loop(done, until, child_then_pair, 0)
-                lax.fori_loop(2 * until - 4, 8 * group + 8, finish, 0)
+                lax.fori_loop(2 * until - 4, 8 * group + 8, finish, 0, unroll=True)
                 put_group(group)
                 done = until
 

time: 41.8 us -> 39.5 us (0.945)
  Pallas kernels: 40.6 us -> 38.4 us
    pallas_call x1, Pallas kernels: 40.6 us -> 38.4 us  [local_fused(): pl.pallas_call(functools.partial(kernel, pulses, beams, span), out_shape=...]
where the time goes in v5:
time: 39.5 us; the launch traced here: 39.3 us
  Pallas kernels  38.4 us (97%)
  local copies, waits for them, and re-layouts  0.97 us (2%)
    pallas_call x1, Pallas kernels, local_fused(): pl.pallas_call(functools.partial(kernel, pulses, beams, span), out_shape=...  38.4 us
    unnamed x1, local copies, waits for them, and re-layouts  0.97 us

profile of v5, /device:TPU:0, one launch (start us, length us, event | category | flops | bytes accessed | tf_op | source)
XLA Modules:
  0.0 39.3 jit_solution(8103642165532209397)
XLA Ops:
  0.0 38.4 %shard_map.91 = f32[2,16,8192]{2,1,0:T(8,128)S(1)} custom-call(bf16[1024,128]{1,0:T(8,128)(2,1)} %bitcast.1, f32[2,128]{1,0:T(2,128)} %refs_1_.1, f32[8,16]{1,0:T(8,128)} %refs_2_.1, s32[8,16]{1,0:T(8,128)} %refs_3_.1, s32[4,2,2,16]{3,2,1,0:T(2,128)} %refs_4_.1, s32[4,2,2,16]{3,2,1,0:T(2,128)} %refs_5_.1, f32[4,2,2,16]{3,2,1,0:T(2,128)} %refs_6_.1, ...), custom_call_target="tpu_custom_call" | custom-call | tf_op jit(solution)/shard_map/pallas_call | solution.py:630
  38.4 1.0 %copy.11 = f32[2,16,8192]{2,1,0:T(8,128)} copy(f32[2,16,8192]{2,1,0:T(8,128)S(1)} %shard_map.91) | data formatting | bytes 2097152
